TPU v7x, 512 devices: a whole 4x8x8 slice. The times are simulated.
512 devices in a mesh: sec: 32 (over y, z_hi, core), sub: 16 (over z_lo, x).
Axes of the slice: x: 4, y: 8, z: 8 (z_hi: 2, z_lo: 4; z = z_hi * 4 + z_lo), core: 2. Of those that a mesh axis runs over, the one named last changes fastest.
Arguments:
- forcing: float32 [32, 192, 64, 128], P('sec', 'sub'), may hold values from -60 to 60
- coupling: float32 [32, 192, 64, 128], P('sec', 'sub'), may hold values from -0.6 to 0.6
- diag_pair: float32 [32, 192, 64, 128], P('sec', 'sub'), may hold values from -1 to 9
- side: float32 [32, 192, 32], P('sec', 'sub'), may hold values from -1 to -0.3
- basis: float32 [32, 1024, 768], P('sec', 'sub'), may hold values from -0.21875 to 0.21875
- coarse_inverse: float32 [32, 1024, 1024], P('sec', 'sub'), may hold values from -0.05 to 0.3
Outputs:
- solution: float32 [32, 192, 64, 128], P('sec', 'sub')
All inputs are finite; a program needn't handle non-finite values.
Results may differ from a plain program's by a relative error of at most 0.0001.
Values sent between devices are 32-bit elements; how exact they have to be, the bound alone decides.
No kernel may reach another device: no remote copies, remote signals or barrier semaphores. Data moves between devices by JAX's collectives and lax.ppermute only.
A program may use at most 64 MiB of HBM per device.

v0:
```python
import jax
import jax.numpy as jnp
from jax import lax
from jax.sharding import PartitionSpec as P

SWEEPS = 4
ITERS = 2
PRECISE = lax.Precision.HIGHEST


def extended(block, sides, width):
    for axis, dim in sides:
        count = lax.axis_size(axis)
        forward = [(i, i + 1) for i in range(count - 1)]
        backward = [(target, source) for source, target in forward]
        low = lax.ppermute(
            lax.slice_in_dim(block, block.shape[dim] - width, None, axis=dim), axis, forward
        )
        high = lax.ppermute(lax.slice_in_dim(block, 0, width, axis=dim), axis, backward)
        block = jnp.concatenate([low, block, high], axis=dim)
    return block


def from_behind(value, axis, steps):
    count = lax.axis_size(axis)
    initial, last = (max(0, -steps), min(count, count - steps))
    return lax.ppermute(value, axis, [(source, source + steps) for source in range(initial, last)])


def tile_apply(tile_set, vector):
    return jnp.einsum("bij,bjc->bic", tile_set, vector, precision=PRECISE)


def couple(coupling, diagonal, centre, before, after):
    return tile_apply(diagonal, centre) + tile_apply(
        coupling, jnp.concatenate([before, after], axis=1)
    )


def chain_apply(coupling, diagonal, vector):
    zero_block = jnp.zeros_like(vector[:1])
    before = jnp.concatenate([zero_block, vector[:-1]], axis=0)
    after = jnp.concatenate([vector[1:], zero_block], axis=0)
    return couple(coupling, diagonal, vector, before, after)


def add_faces(linear, sides, below, above):
    face_rows = sides.shape[-1] // 2
    node_count = linear.shape[1]
    lower_term = sides[:, :face_rows, None] * below
    upper_term = sides[:, face_rows:, None] * above
    return jnp.concatenate(
        [
            linear[:, :face_rows] + lower_term,
            linear[:, face_rows : node_count - face_rows],
            linear[:, node_count - face_rows :] + upper_term,
        ],
        axis=1,
    )


def local_sweeps(residual_ext, coupling_ext, diagonal_ext, inverse_ext):
    update = tile_apply(inverse_ext, residual_ext)
    for sweep_index in range(SWEEPS - 1):
        update = update + tile_apply(
            inverse_ext, residual_ext - chain_apply(coupling_ext, diagonal_ext, update)
        )
    return update[1:-1]


def project(basis_rows, field):
    return jnp.dot(basis_rows, field.reshape(-1, field.shape[-1]), precision=PRECISE)


def expand(basis_rows, correction, target_shape):
    spread = lax.dot_general(basis_rows, correction, (((0,), (0,)), ((), ())), precision=PRECISE)
    return spread.reshape(target_shape)


def fold_rows(inverse_rows, segment):
    return jnp.dot(inverse_rows, segment, precision=PRECISE)


def coarse_direct(basis_rows, inverse_rows, residual):
    projected = project(basis_rows, residual)
    return fold_rows(inverse_rows, lax.all_gather(projected, "sub", axis=0, tiled=True))


def operate(update, coupling, diagonal, sides):
    update_ext = extended(update, (("sub", 0),), 1)
    linear = couple(coupling, diagonal, update, update_ext[:-2], update_ext[2:])
    face_rows = sides.shape[-1] // 2
    node_count = update.shape[1]
    north_face = update[:, node_count - face_rows :, :]
    south_face = update[:, :face_rows, :]
    below = from_behind(north_face, "sec", 1)
    above = from_behind(south_face, "sec", -1)
    return add_faces(linear, sides, below, above)


def step_length(image, residual):
    numerator, denominator = lax.psum(
        (jnp.sum(image * residual, axis=(0, 1)), jnp.sum(image * image, axis=(0, 1))),
        ("sec", "sub"),
    )
    return numerator / denominator


def shards(forcing, coupling, diag_pair, side, basis, coarse_inverse):
    residual = forcing[0]
    couplings = coupling[0]
    pairs = diag_pair[0]
    sides = side[0]
    basis_rows = basis[0]
    inverse_rows = coarse_inverse[0]
    node_count = residual.shape[1]
    stacked = jnp.concatenate([couplings, pairs], axis=2)
    stacked_ext = extended(stacked, (("sub", 0),), 1)
    coupling_ext = stacked_ext[:, :, : 2 * node_count]
    diagonal_ext = stacked_ext[:, :, 2 * node_count : 3 * node_count]
    inverse_ext = stacked_ext[:, :, 3 * node_count :]
    diagonal_own = pairs[:, :, :node_count]
    solution = jnp.zeros_like(residual)
    for iteration in range(ITERS):
        correction = coarse_direct(basis_rows, inverse_rows, residual)
        residual_ext = extended(residual, (("sub", 0),), 1)
        local_part = local_sweeps(residual_ext, coupling_ext, diagonal_ext, inverse_ext)
        update = local_part + expand(basis_rows, correction, residual.shape)
        image = operate(update, couplings, diagonal_own, sides)
        step_size = step_length(image, residual)
        solution = solution + step_size * update
        residual = residual - step_size * image
    return solution[None]


def solution(mesh):
    placed = (
        P("sec", "sub", None, None),
        P("sec", "sub", None, None),
        P("sec", "sub", None, None),
        P("sec", "sub", None),
        P("sec", "sub", None),
        P("sec", "sub", None),
    )
    return jax.shard_map(
        shards, mesh=mesh, in_specs=placed, out_specs=P("sec", "sub", None, None), check_vma=False
    )
```

profile of v0, /device:TPU:1, one launch (start us, length us, event | category | flops | bytes accessed | tf_op | source)
XLA Modules:
  0.0 371.0 jit_solution(13853140546099342183)
XLA Ops:
  0.0 1.4 slice_bitcast_fusion.1
  1.4 3.9 %collective-permute-start.2 = (f32[1,64,128]{2,1,0:T(8,128)}, f32[1,64,128]{2,1,0:T(8,128)S(1)}, u32[]{:S(2)}, u32[]{:S(2)}) collective-permute-start(f32[1,64,128]{2,1,0:T(8,128)} %get-tuple-element.43), channel_id=1, source_target_pairs={{0,1},{1,2},{2,3},{3,4},{4,5},{5,6},{6,7},{7,8},{8,9},{9,10},{10,1... | collective-permute-start | bytes 98312 | tf_op jit(solution)/shard_map/ppermute | solution.py:16
  5.4 1.3 collective-permute-start.3
  7.6 4.6 %collective-permute-start = (f32[1,64,256]{2,1,0:T(8,128)S(1)}, f32[1,64,256]{2,1,0:T(8,128)}, u32[]{:S(2)}, u32[]{:S(2)}) collective-permute-start(f32[1,64,256]{2,1,0:T(8,128)S(1)} %get-tuple-element.13), channel_id=1, source_target_pairs={{0,1},{1,2},{2,3},{3,4},{4,5},{5,6},{6,7},{7,8},{8,9},{9,10},{10,1... | collective-permute-start | bytes 196616 | tf_op jit(solution)/shard_map/ppermute | solution.py:16
  12.2 1.3 collective-permute-start.1
  13.9 41.7 %all_gather.6 = f32[1024,128]{1,0:T(8,128)S(1)} all-gather(f32[64,128]{1,0:T(8,128)S(1)} %fusion.90), channel_id=1, replica_groups=mesh['sec'=32,'sub'=16] {'sub'}, dimensions={0}, use_global_device_ids=true | all-gather | bytes 557056 | tf_op jit(solution)/shard_map/all_gather | solution.py:86
  55.6 1.0 fusion.85
  67.2 1.3 collective-permute-start.4
  68.5 1.3 collective-permute-start.5
  69.8 16.4 %collective-permute-start.6 = (f32[12,16,128]{2,1,0:T(8,128)S(1)}, f32[12,16,128]{2,1,0:T(8,128)S(1)}, u32[]{:S(2)}, u32[]{:S(2)}) collective-permute-start(f32[12,16,128]{2,1,0:T(8,128)S(1)} %get-tuple-element.39), channel_id=1, source_target_pairs={{0,16},{16,32},{32,48},{48,64},{64,80},{80,96},{96,112},{112,128},... | collective-permute-start | bytes 294920 | tf_op jit(solution)/shard_map/ppermute | solution.py:27
  86.3 1.9 collective-permute-start.7
  89.7 6.4 %collective-permute-done.7 = f32[12,16,128]{2,1,0:T(8,128)S(1)} collective-permute-done((f32[12,16,128]{2,1,0:T(8,128)S(1)}, f32[12,16,128]{2,1,0:T(8,128)S(1)}, u32[]{:S(2)}, u32[]{:S(2)}) %collective-permute-start.7) | collective-permute-done | bytes 98336 | tf_op jit(solution)/shard_map/ppermute | solution.py:27
  96.9 97.6 %all-reduce.13 = (f32[128]{0:T(128)S(1)}, f32[128]{0:T(128)S(1)}) all-reduce(f32[128]{0:T(128)S(1)} %get-tuple-element.8, f32[128]{0:T(128)S(1)} %get-tuple-element.7), channel_id=1, replica_groups=mesh['sec'=32,'sub'=16] {'sec','sub'}, use_global_device_ids=true, to_apply=%region_1.0 | all-reduce | flops 256 | bytes 2048 | tf_op jit(solution)/shard_map/psum | solution.py:102
  194.6 1.0 multiply_subtract_fusion
  196.1 2.2 collective-permute-start.8
  198.4 1.3 collective-permute-start.9
  199.7 35.9 %all_gather.7 = f32[1024,128]{1,0:T(8,128)S(1)} all-gather(f32[64,128]{1,0:T(8,128)S(1)} %convolution_bitcast_fusion.2), channel_id=1, replica_groups=mesh['sec'=32,'sub'=16] {'sub'}, dimensions={0}, use_global_device_ids=true | all-gather | bytes 557056 | tf_op jit(solution)/shard_map/all_gather | solution.py:86
  235.5 1.0 fusion.83
  246.2 1.3 collective-permute-start.10
  247.5 1.3 collective-permute-start.11
  248.9 13.5 %collective-permute-start.12 = (f32[12,16,128]{2,1,0:T(8,128)S(1)}, f32[12,16,128]{2,1,0:T(8,128)S(1)}, u32[]{:S(2)}, u32[]{:S(2)}) collective-permute-start(f32[12,16,128]{2,1,0:T(8,128)S(1)} %get-tuple-element.29), channel_id=1, source_target_pairs={{0,16},{16,32},{32,48},{48,64},{64,80},{80,96},{96,112},{112,128},... | collective-permute-start | bytes 294920 | tf_op jit(solution)/shard_map/ppermute | solution.py:27
  262.4 1.9 collective-permute-start.13
  265.1 7.6 %collective-permute-done.13 = f32[12,16,128]{2,1,0:T(8,128)S(1)} collective-permute-done((f32[12,16,128]{2,1,0:T(8,128)S(1)}, f32[12,16,128]{2,1,0:T(8,128)S(1)}, u32[]{:S(2)}, u32[]{:S(2)}) %collective-permute-start.13) | collective-permute-done | bytes 98336 | tf_op jit(solution)/shard_map/ppermute | solution.py:27
  273.0 96.6 %all-reduce.12 = (f32[128]{0:T(128)S(1)}, f32[128]{0:T(128)S(1)}) all-reduce(f32[128]{0:T(128)S(1)} %get-tuple-element.6, f32[128]{0:T(128)S(1)} %get-tuple-element.5), channel_id=1, replica_groups=mesh['sec'=32,'sub'=16] {'sec','sub'}, use_global_device_ids=true, to_apply=%region_5.0 | all-reduce | flops 256 | bytes 2048 | tf_op jit(solution)/shard_map/psum | solution.py:102
  (97 shorter events, 26.5 us)
Async XLA Ops:
  0.0 55.6 %copy-start = (f32[1,64,1024]{2,1,0:T(8,128)S(1)}, f32[1,64,1024]{2,1,0:T(8,128)}, u32[]{:S(2)}) copy-start(f32[1,64,1024]{2,1,0:T(8,128)} %param.11) | copy-start | bytes 786436
  1.4 57.8 %collective-permute-start.2 = (f32[1,64,128]{2,1,0:T(8,128)}, f32[1,64,128]{2,1,0:T(8,128)S(1)}, u32[]{:S(2)}, u32[]{:S(2)}) collective-permute-start(f32[1,64,128]{2,1,0:T(8,128)} %get-tuple-element.43), channel_id=1, source_target_pairs={{0,1},{1,2},{2,3},{3,4},{4,5},{5,6},{6,7},{7,8},{8,9},{9,10},{10,1... | collective-permute-start | bytes 98312 | tf_op jit(solution)/shard_map/ppermute | solution.py:16
  5.4 53.9 %collective-permute-start.3 = (f32[1,64,128]{2,1,0:T(8,128)S(1)}, f32[1,64,128]{2,1,0:T(8,128)S(1)}, u32[]{:S(2)}, u32[]{:S(2)}) collective-permute-start(f32[1,64,128]{2,1,0:T(8,128)S(1)} %get-tuple-element.44), channel_id=1, source_target_pairs={{1,0},{2,1},{3,2},{4,3},{5,4},{6,5},{7,6},{8,7},{9,8},{10,9},{11,1... | collective-permute-start | bytes 98312 | tf_op jit(solution)/shard_map/ppermute | solution.py:19
  6.7 6.8 %copy-start.11 = (f32[1,12,32]{2,0,1:T(1,128)S(1)}, f32[1,12,32]{2,0,1:T(1,128)}, u32[]{:S(2)}) copy-start(f32[1,12,32]{2,0,1:T(1,128)} %param.9) | copy-start | bytes 4612
  6.7 6.8 %copy-start.1 = (f32[1,12,64,128]{3,2,1,0:T(8,128)S(1)}, f32[1,12,64,128]{3,2,1,0:T(8,128)}, u32[]{:S(2)}) copy-start(f32[1,12,64,128]{3,2,1,0:T(8,128)} %param.6) | copy-start | bytes 1179652
  6.7 6.8 %copy-start.4 = (f32[1,64,768]{2,1,0:T(8,128)S(1)}, f32[1,64,768]{2,1,0:T(8,128)}, u32[]{:S(2)}) copy-start(f32[1,64,768]{2,1,0:T(8,128)} %param.10) | copy-start | bytes 589828
  7.6 49.8 %collective-permute-start = (f32[1,64,256]{2,1,0:T(8,128)S(1)}, f32[1,64,256]{2,1,0:T(8,128)}, u32[]{:S(2)}, u32[]{:S(2)}) collective-permute-start(f32[1,64,256]{2,1,0:T(8,128)S(1)} %get-tuple-element.13), channel_id=1, source_target_pairs={{0,1},{1,2},{2,3},{3,4},{4,5},{5,6},{6,7},{7,8},{8,9},{9,10},{10,1... | collective-permute-start | bytes 196616 | tf_op jit(solution)/shard_map/ppermute | solution.py:16
  12.2 45.2 %collective-permute-start.1 = (f32[1,64,256]{2,1,0:T(8,128)S(1)}, f32[1,64,256]{2,1,0:T(8,128)}, u32[]{:S(2)}, u32[]{:S(2)}) collective-permute-start(f32[1,64,256]{2,1,0:T(8,128)S(1)} %get-tuple-element.14), channel_id=1, source_target_pairs={{1,0},{2,1},{3,2},{4,3},{5,4},{6,5},{7,6},{8,7},{9,8},{10,9},{11,1... | collective-permute-start | bytes 196616 | tf_op jit(solution)/shard_map/ppermute | solution.py:19
  57.2 1.1 copy-start.3
  67.2 21.0 %collective-permute-start.4 = (f32[1,64,128]{2,1,0:T(8,128)S(1)}, f32[1,64,128]{2,1,0:T(8,128)S(1)}, u32[]{:S(2)}, u32[]{:S(2)}) collective-permute-start(f32[1,64,128]{2,1,0:T(8,128)S(1)} %get-tuple-element.41), channel_id=1, source_target_pairs={{0,1},{1,2},{2,3},{3,4},{4,5},{5,6},{6,7},{7,8},{8,9},{9,10},{10,1... | collective-permute-start | bytes 98312 | tf_op jit(solution)/shard_map/ppermute | solution.py:16
  68.5 19.7 %collective-permute-start.5 = (f32[1,64,128]{2,1,0:T(8,128)S(1)}, f32[1,64,128]{2,1,0:T(8,128)S(1)}, u32[]{:S(2)}, u32[]{:S(2)}) collective-permute-start(f32[1,64,128]{2,1,0:T(8,128)S(1)} %get-tuple-element.42), channel_id=1, source_target_pairs={{1,0},{2,1},{3,2},{4,3},{5,4},{6,5},{7,6},{8,7},{9,8},{10,9},{11,1... | collective-permute-start | bytes 98312 | tf_op jit(solution)/shard_map/ppermute | solution.py:19
  69.8 19.9 %collective-permute-start.6 = (f32[12,16,128]{2,1,0:T(8,128)S(1)}, f32[12,16,128]{2,1,0:T(8,128)S(1)}, u32[]{:S(2)}, u32[]{:S(2)}) collective-permute-start(f32[12,16,128]{2,1,0:T(8,128)S(1)} %get-tuple-element.39), channel_id=1, source_target_pairs={{0,16},{16,32},{32,48},{48,64},{64,80},{80,96},{96,112},{112,128},... | collective-permute-start | bytes 294920 | tf_op jit(solution)/shard_map/ppermute | solution.py:27
  86.3 9.8 %collective-permute-start.7 = (f32[12,16,128]{2,1,0:T(8,128)S(1)}, f32[12,16,128]{2,1,0:T(8,128)S(1)}, u32[]{:S(2)}, u32[]{:S(2)}) collective-permute-start(f32[12,16,128]{2,1,0:T(8,128)S(1)} %get-tuple-element.40), channel_id=1, source_target_pairs={{16,0},{32,16},{48,32},{64,48},{80,64},{96,80},{112,96},{128,112},... | collective-permute-start | bytes 294920 | tf_op jit(solution)/shard_map/ppermute | solution.py:27
  194.6 1.1 copy-start.12
  194.6 1.1 copy-start.6
  194.6 1.1 copy-start.8
  194.6 1.1 copy-start.10
  196.1 41.8 %collective-permute-start.8 = (f32[1,64,128]{2,1,0:T(8,128)S(1)}, f32[1,64,128]{2,1,0:T(8,128)S(1)}, u32[]{:S(2)}, u32[]{:S(2)}) collective-permute-start(f32[1,64,128]{2,1,0:T(8,128)S(1)} %get-tuple-element.33), channel_id=1, source_target_pairs={{0,1},{1,2},{2,3},{3,4},{4,5},{5,6},{6,7},{7,8},{8,9},{9,10},{10,1... | collective-permute-start | bytes 98312 | tf_op jit(solution)/shard_map/ppermute | solution.py:16
  198.4 39.6 %collective-permute-start.9 = (f32[1,64,128]{2,1,0:T(8,128)S(1)}, f32[1,64,128]{2,1,0:T(8,128)S(1)}, u32[]{:S(2)}, u32[]{:S(2)}) collective-permute-start(f32[1,64,128]{2,1,0:T(8,128)S(1)} %get-tuple-element.34), channel_id=1, source_target_pairs={{1,0},{2,1},{3,2},{4,3},{5,4},{6,5},{7,6},{8,7},{9,8},{10,9},{11,1... | collective-permute-start | bytes 98312 | tf_op jit(solution)/shard_map/ppermute | solution.py:19
  244.7 1.0 copy-start.9
  246.2 18.0 %collective-permute-start.10 = (f32[1,64,128]{2,1,0:T(8,128)S(1)}, f32[1,64,128]{2,1,0:T(8,128)S(1)}, u32[]{:S(2)}, u32[]{:S(2)}) collective-permute-start(f32[1,64,128]{2,1,0:T(8,128)S(1)} %get-tuple-element.31), channel_id=1, source_target_pairs={{0,1},{1,2},{2,3},{3,4},{4,5},{5,6},{6,7},{7,8},{8,9},{9,10},{10,1... | collective-permute-start | bytes 98312 | tf_op jit(solution)/shard_map/ppermute | solution.py:16
  247.5 16.7 %collective-permute-start.11 = (f32[1,64,128]{2,1,0:T(8,128)S(1)}, f32[1,64,128]{2,1,0:T(8,128)S(1)}, u32[]{:S(2)}, u32[]{:S(2)}) collective-permute-start(f32[1,64,128]{2,1,0:T(8,128)S(1)} %get-tuple-element.32), channel_id=1, source_target_pairs={{1,0},{2,1},{3,2},{4,3},{5,4},{6,5},{7,6},{8,7},{9,8},{10,9},{11,1... | collective-permute-start | bytes 98312 | tf_op jit(solution)/shard_map/ppermute | solution.py:19
  248.9 16.2 %collective-permute-start.12 = (f32[12,16,128]{2,1,0:T(8,128)S(1)}, f32[12,16,128]{2,1,0:T(8,128)S(1)}, u32[]{:S(2)}, u32[]{:S(2)}) collective-permute-start(f32[12,16,128]{2,1,0:T(8,128)S(1)} %get-tuple-element.29), channel_id=1, source_target_pairs={{0,16},{16,32},{32,48},{48,64},{64,80},{80,96},{96,112},{112,128},... | collective-permute-start | bytes 294920 | tf_op jit(solution)/shard_map/ppermute | solution.py:27
  262.4 10.4 %collective-permute-start.13 = (f32[12,16,128]{2,1,0:T(8,128)S(1)}, f32[12,16,128]{2,1,0:T(8,128)S(1)}, u32[]{:S(2)}, u32[]{:S(2)}) collective-permute-start(f32[12,16,128]{2,1,0:T(8,128)S(1)} %get-tuple-element.30), channel_id=1, source_target_pairs={{16,0},{32,16},{48,32},{64,48},{80,64},{96,80},{112,96},{128,112},... | collective-permute-start | bytes 294920 | tf_op jit(solution)/shard_map/ppermute | solution.py:27
  (4 other events, 2.9 us)
where the time goes:
time: 372 us; the launch traced here: 371 us
  blocking collectives  272 us (73%)
  starting transfers between devices  53.5 us (14%)
  matrix products  20.1 us (5%)
  waiting for transfers between devices  14.1 us (4%)
  local copies, waits for them, and re-layouts  6.39 us (2%)
  other arithmetic  4.42 us (1%)
    psum x2, blocking collectives, step_length(): lax.psum((jnp.sum(image * residual, axis=(0, 1)), jnp.sum(image * image,...  194 us
    all_gather x2, blocking collectives, coarse_direct(): lax.all_gather(projected, 'sub', axis=0, tiled=True)  77.6 us
    ppermute x4, starting transfers between devices, from_behind(): lax.ppermute(value, axis, [(source, source + steps) for source in range(i...  33.7 us
    dot_general x24, matrix products, tile_apply(): return jnp.einsum('bij,bjc->bic', tile_set, vector, precision=PRECISE)  16.5 us
    ppermute x4, waiting for transfers between devices, from_behind(): lax.ppermute(value, axis, [(source, source + steps) for source in range(i...  14 us
    ppermute x5, starting transfers between devices, extended(): lax.ppermute(lax.slice_in_dim(block, block.shape[dim] - width, None, axis...  13.3 us
  transfers between devices with their start and end apart: 14, of which 2 were waited for; matrix products, arithmetic and copies ran while one was open for 2% of the time, Pallas kernels for 0%

commit v1 on v0

--- a/solution.py
+++ b/solution.py
@@ -6,6 +6,11 @@
 SWEEPS = 4
 ITERS = 2
 PRECISE = lax.Precision.HIGHEST
+
+
+def all_by_exchange(x, mesh_axis, dim):
+    stack = jnp.stack([x] * lax.axis_size(mesh_axis))
+    return jnp.concatenate(lax.all_to_all(stack, mesh_axis, 0, 0), axis=dim)
 
 
 def extended(block, sides, width):
@@ -83,7 +88,7 @@
 
 def coarse_direct(basis_rows, inverse_rows, residual):
     projected = project(basis_rows, residual)
-    return fold_rows(inverse_rows, lax.all_gather(projected, "sub", axis=0, tiled=True))
+    return fold_rows(inverse_rows, all_by_exchange(projected, "sub", 0))
 
 
 def operate(update, coupling, diagonal, sides):

time: 372 us -> 325 us (0.87)
  blocking collectives: 272 us -> 203 us
  waiting for transfers between devices: 14.1 us -> 23.8 us
  starting transfers between devices: 53.5 us -> 63 us
    all_gather x2 -> x0, blocking collectives: 77.6 us -> none  [coarse_direct(): lax.all_gather(projected, 'sub', axis=0, tiled=True)]
    all_to_all x0 -> x2, starting transfers between devices: none -> 17.4 us  [all_by_exchange(): return jnp.concatenate(lax.all_to_all(stack, mesh_axis, 0, 0), axis=dim)]
    ppermute x4, starting transfers between devices: 33.7 us -> 23 us  [from_behind(): lax.ppermute(value, axis, [(source, source + steps) for source in range(i...]
    all_to_all x0 -> x2, waiting for transfers between devices: none -> 9.65 us  [all_by_exchange(): return jnp.concatenate(lax.all_to_all(stack, mesh_axis, 0, 0), axis=dim)]
    psum x2, blocking collectives: 194 us -> 203 us  [step_length(): lax.psum((jnp.sum(image * residual, axis=(0, 1)), jnp.sum(image * image,...]
  transfers between devices with their start and end apart: 14 -> 16, of which waited for: 2 -> 4; matrix products, arithmetic and copies ran while one was open for 2% -> 7% of each run, Pallas kernels for 0% -> 0%
where the time goes in v1:
time: 325 us; the launch traced here: 324 us
  blocking collectives  203 us (62%)
  starting transfers between devices  63 us (19%)
  waiting for transfers between devices  23.8 us (7%)
  matrix products  23.7 us (7%)
  local copies, waits for them, and re-layouts  5.84 us (2%)
  other arithmetic  3.61 us (1%)
    psum x2, blocking collectives, step_length(): lax.psum((jnp.sum(image * residual, axis=(0, 1)), jnp.sum(image * image,...  203 us
    ppermute x4, starting transfers between devices, from_behind(): lax.ppermute(value, axis, [(source, source + steps) for source in range(i...  23 us
    dot_general x24, matrix products, tile_apply(): return jnp.einsum('bij,bjc->bic', tile_set, vector, precision=PRECISE)  18.1 us
    all_to_all x2, starting transfers between devices, all_by_exchange(): return jnp.concatenate(lax.all_to_all(stack, mesh_axis, 0, 0), axis=dim)  17.4 us
    ppermute x5, starting transfers between devices, extended(): lax.ppermute(lax.slice_in_dim(block, block.shape[dim] - width, None, axis...  16.2 us
    ppermute x4, waiting for transfers between devices, from_behind(): lax.ppermute(value, axis, [(source, source + steps) for source in range(i...  14.1 us
    all_to_all x2, waiting for transfers between devices, all_by_exchange(): return jnp.concatenate(lax.all_to_all(stack, mesh_axis, 0, 0), axis=dim)  9.65 us
  transfers between devices with their start and end apart: 16, of which 4 were waited for; matrix products, arithmetic and copies ran while one was open for 7% of the time, Pallas kernels for 0%

profile of v1, /device:TPU:1, one launch (start us, length us, event | category | flops | bytes accessed | tf_op | source)
XLA Modules:
  0.0 324.0 jit_solution(15447986709908389980)
XLA Ops:
  0.8 3.9 %collective-permute-start.2 = (f32[1,64,128]{2,1,0:T(8,128)S(1)}, f32[1,64,128]{2,1,0:T(8,128)S(1)}, u32[]{:S(2)}, u32[]{:S(2)}) collective-permute-start(f32[1,64,128]{2,1,0:T(8,128)S(1)} %get-tuple-element.43), channel_id=1, source_target_pairs={{0,1},{1,2},{2,3},{3,4},{4,5},{5,6},{6,7},{7,8},{8,9},{9,10},{10,1... | collective-permute-start | bytes 98312 | tf_op jit(solution)/shard_map/ppermute | solution.py:21
  7.0 4.0 %collective-permute-start = (f32[1,64,256]{2,1,0:T(8,128)S(1)}, f32[1,64,256]{2,1,0:T(8,128)S(1)}, u32[]{:S(2)}, u32[]{:S(2)}) collective-permute-start(f32[1,64,256]{2,1,0:T(8,128)S(1)} %get-tuple-element.13), channel_id=1, source_target_pairs={{0,1},{1,2},{2,3},{3,4},{4,5},{5,6},{6,7},{7,8},{8,9},{9,10},{10,1... | collective-permute-start | bytes 196616 | tf_op jit(solution)/shard_map/ppermute | solution.py:21
  11.0 1.3 collective-permute-start.1
  13.5 12.4 %all-to-all-start = ((f32[16,64,128]{2,1,0:T(8,128)}), f32[16,64,128]{2,1,0:T(8,128)}, u32[]{:S(2)}, u32[]{:S(2)}) async-start(f32[16,64,128]{2,1,0:T(8,128)} %stack.4), calls=%async_computation | async-start | bytes 1048576 | tf_op jit(solution)/shard_map/all_to_all | solution.py:13
  32.8 1.4 fusion.77
  34.3 4.5 %all-to-all-done = f32[16,64,128]{2,1,0:T(8,128)} async-done(((f32[16,64,128]{2,1,0:T(8,128)}), f32[16,64,128]{2,1,0:T(8,128)}, u32[]{:S(2)}, u32[]{:S(2)}) %all-to-all-start) | async-done | bytes 524320 | tf_op jit(solution)/shard_map/all_to_all | solution.py:13
  38.8 2.0 fusion.85
  43.9 2.2 collective-permute-start.4
  46.1 1.3 collective-permute-start.5
  47.5 11.7 %collective-permute-start.6 = (f32[12,16,128]{2,1,0:T(8,128)S(1)}, f32[12,16,128]{2,1,0:T(8,128)S(1)}, u32[]{:S(2)}, u32[]{:S(2)}) collective-permute-start(f32[12,16,128]{2,1,0:T(8,128)S(1)} %get-tuple-element.39), channel_id=1, source_target_pairs={{0,16},{16,32},{32,48},{48,64},{64,80},{80,96},{96,112},{112,128},... | collective-permute-start | bytes 294920 | tf_op jit(solution)/shard_map/ppermute | solution.py:32
  59.2 2.1 collective-permute-start.7
  62.1 7.0 %collective-permute-done.7 = f32[12,16,128]{2,1,0:T(8,128)S(1)} collective-permute-done((f32[12,16,128]{2,1,0:T(8,128)S(1)}, f32[12,16,128]{2,1,0:T(8,128)S(1)}, u32[]{:S(2)}, u32[]{:S(2)}) %collective-permute-start.7) | collective-permute-done | bytes 98336 | tf_op jit(solution)/shard_map/ppermute | solution.py:32
  69.4 101.0 %all-reduce.13 = (f32[128]{0:T(128)S(1)}, f32[128]{0:T(128)S(1)}) all-reduce(f32[128]{0:T(128)S(1)} %get-tuple-element.8, f32[128]{0:T(128)S(1)} %get-tuple-element.7), channel_id=1, replica_groups=mesh['sec'=32,'sub'=16] {'sec','sub'}, use_global_device_ids=true, to_apply=%region_1.0 | all-reduce | flops 256 | bytes 2048 | tf_op jit(solution)/shard_map/psum | solution.py:107
  170.5 3.7 %collective-permute-start.8 = (f32[1,64,128]{2,1,0:T(8,128)S(1)}, f32[1,64,128]{2,1,0:T(8,128)S(1)}, u32[]{:S(2)}, u32[]{:S(2)}) collective-permute-start(f32[1,64,128]{2,1,0:T(8,128)S(1)} %get-tuple-element.33), channel_id=1, source_target_pairs={{0,1},{1,2},{2,3},{3,4},{4,5},{5,6},{6,7},{7,8},{8,9},{9,10},{10,1... | collective-permute-start | bytes 98312 | tf_op jit(solution)/shard_map/ppermute | solution.py:21
  174.2 1.3 collective-permute-start.9
  176.8 5.0 %all-to-all-start.1 = ((f32[16,64,128]{2,1,0:T(8,128)}), f32[16,64,128]{2,1,0:T(8,128)}, u32[]{:S(2)}, u32[]{:S(2)}) async-start(f32[16,64,128]{2,1,0:T(8,128)} %stack.5), calls=%async_computation.1 | async-start | bytes 1048576 | tf_op jit(solution)/shard_map/all_to_all | solution.py:13
  188.6 1.4 fusion.71
  190.1 5.1 %all-to-all-done.1 = f32[16,64,128]{2,1,0:T(8,128)} async-done(((f32[16,64,128]{2,1,0:T(8,128)}), f32[16,64,128]{2,1,0:T(8,128)}, u32[]{:S(2)}, u32[]{:S(2)}) %all-to-all-start.1) | async-done | bytes 524320 | tf_op jit(solution)/shard_map/all_to_all | solution.py:13
  195.2 2.0 fusion.83
  199.3 2.3 collective-permute-start.10
  203.0 7.3 %collective-permute-start.12 = (f32[12,16,128]{2,1,0:T(8,128)S(1)}, f32[12,16,128]{2,1,0:T(8,128)S(1)}, u32[]{:S(2)}, u32[]{:S(2)}) collective-permute-start(f32[12,16,128]{2,1,0:T(8,128)S(1)} %get-tuple-element.29), channel_id=1, source_target_pairs={{0,16},{16,32},{32,48},{48,64},{64,80},{80,96},{96,112},{112,128},... | collective-permute-start | bytes 294920 | tf_op jit(solution)/shard_map/ppermute | solution.py:32
  210.3 1.9 collective-permute-start.13
  213.0 7.1 %collective-permute-done.13 = f32[12,16,128]{2,1,0:T(8,128)S(1)} collective-permute-done((f32[12,16,128]{2,1,0:T(8,128)S(1)}, f32[12,16,128]{2,1,0:T(8,128)S(1)}, u32[]{:S(2)}, u32[]{:S(2)}) %collective-permute-start.13) | collective-permute-done | bytes 98336 | tf_op jit(solution)/shard_map/ppermute | solution.py:32
  220.4 102.2 %all-reduce.12 = (f32[128]{0:T(128)S(1)}, f32[128]{0:T(128)S(1)}) all-reduce(f32[128]{0:T(128)S(1)} %get-tuple-element.6, f32[128]{0:T(128)S(1)} %get-tuple-element.5), channel_id=1, replica_groups=mesh['sec'=32,'sub'=16] {'sec','sub'}, use_global_device_ids=true, to_apply=%region_5.0 | all-reduce | flops 256 | bytes 2048 | tf_op jit(solution)/shard_map/psum | solution.py:107
  (101 shorter events, 28.9 us)
Async XLA Ops:
  0.0 38.8 %copy-start = (f32[1,64,1024]{2,1,0:T(8,128)S(1)}, f32[1,64,1024]{2,1,0:T(8,128)}, u32[]{:S(2)}) copy-start(f32[1,64,1024]{2,1,0:T(8,128)} %param.11) | copy-start | bytes 786436
  0.8 25.3 %collective-permute-start.2 = (f32[1,64,128]{2,1,0:T(8,128)S(1)}, f32[1,64,128]{2,1,0:T(8,128)S(1)}, u32[]{:S(2)}, u32[]{:S(2)}) collective-permute-start(f32[1,64,128]{2,1,0:T(8,128)S(1)} %get-tuple-element.43), channel_id=1, source_target_pairs={{0,1},{1,2},{2,3},{3,4},{4,5},{5,6},{6,7},{7,8},{8,9},{9,10},{10,1... | collective-permute-start | bytes 98312 | tf_op jit(solution)/shard_map/ppermute | solution.py:21
  4.8 21.3 %collective-permute-start.3 = (f32[1,64,128]{2,1,0:T(8,128)S(1)}, f32[1,64,128]{2,1,0:T(8,128)S(1)}, u32[]{:S(2)}, u32[]{:S(2)}) collective-permute-start(f32[1,64,128]{2,1,0:T(8,128)S(1)} %get-tuple-element.44), channel_id=1, source_target_pairs={{1,0},{2,1},{3,2},{4,3},{5,4},{6,5},{7,6},{8,7},{9,8},{10,9},{11,1... | collective-permute-start | bytes 98312 | tf_op jit(solution)/shard_map/ppermute | solution.py:24
  6.1 6.2 %copy-start.1 = (f32[1,12,64,128]{3,2,1,0:T(8,128)S(1)}, f32[1,12,64,128]{3,2,1,0:T(8,128)}, u32[]{:S(2)}) copy-start(f32[1,12,64,128]{3,2,1,0:T(8,128)} %param.6) | copy-start | bytes 1179652
  6.1 6.2 %copy-start.5 = (f32[1,64,768]{2,1,0:T(8,128)S(1)}, f32[1,64,768]{2,1,0:T(8,128)}, u32[]{:S(2)}) copy-start(f32[1,64,768]{2,1,0:T(8,128)} %param.10) | copy-start | bytes 589828
  7.0 19.0 %collective-permute-start = (f32[1,64,256]{2,1,0:T(8,128)S(1)}, f32[1,64,256]{2,1,0:T(8,128)S(1)}, u32[]{:S(2)}, u32[]{:S(2)}) collective-permute-start(f32[1,64,256]{2,1,0:T(8,128)S(1)} %get-tuple-element.13), channel_id=1, source_target_pairs={{0,1},{1,2},{2,3},{3,4},{4,5},{5,6},{6,7},{7,8},{8,9},{9,10},{10,1... | collective-permute-start | bytes 196616 | tf_op jit(solution)/shard_map/ppermute | solution.py:21
  11.0 15.0 %collective-permute-start.1 = (f32[1,64,256]{2,1,0:T(8,128)S(1)}, f32[1,64,256]{2,1,0:T(8,128)S(1)}, u32[]{:S(2)}, u32[]{:S(2)}) collective-permute-start(f32[1,64,256]{2,1,0:T(8,128)S(1)} %get-tuple-element.14), channel_id=1, source_target_pairs={{1,0},{2,1},{3,2},{4,3},{5,4},{6,5},{7,6},{8,7},{9,8},{10,9},{11,1... | collective-permute-start | bytes 196616 | tf_op jit(solution)/shard_map/ppermute | solution.py:24
  13.5 12.4 %copy-start.11 = (f32[1,12,32]{2,0,1:T(1,128)S(1)}, f32[1,12,32]{2,0,1:T(1,128)}, u32[]{:S(2)}) copy-start(f32[1,12,32]{2,0,1:T(1,128)} %param.9) | copy-start | bytes 4612
  13.5 12.5 %copy-start.2 = (f32[1,12,64,128]{3,2,1,0:T(8,128)S(1)}, f32[1,12,64,128]{3,2,1,0:T(8,128)}, u32[]{:S(2)}) copy-start(f32[1,12,64,128]{3,2,1,0:T(8,128)} %param.8) | copy-start | bytes 1179652
  13.5 12.5 %copy-start.3 = (f32[1,12,64,128]{3,2,1,0:T(8,128)S(1)}, f32[1,12,64,128]{3,2,1,0:T(8,128)}, u32[]{:S(2)}) copy-start(f32[1,12,64,128]{3,2,1,0:T(8,128)} %param.7) | copy-start | bytes 1179652
  13.5 25.3 %all-to-all-start = ((f32[16,64,128]{2,1,0:T(8,128)}), f32[16,64,128]{2,1,0:T(8,128)}, u32[]{:S(2)}, u32[]{:S(2)}) async-start(f32[16,64,128]{2,1,0:T(8,128)} %stack.4), calls=%async_computation | async-start | bytes 1048576 | tf_op jit(solution)/shard_map/all_to_all | solution.py:13
  43.9 17.4 %collective-permute-start.4 = (f32[1,64,128]{2,1,0:T(8,128)S(1)}, f32[1,64,128]{2,1,0:T(8,128)S(1)}, u32[]{:S(2)}, u32[]{:S(2)}) collective-permute-start(f32[1,64,128]{2,1,0:T(8,128)S(1)} %get-tuple-element.41), channel_id=1, source_target_pairs={{0,1},{1,2},{2,3},{3,4},{4,5},{5,6},{6,7},{7,8},{8,9},{9,10},{10,1... | collective-permute-start | bytes 98312 | tf_op jit(solution)/shard_map/ppermute | solution.py:21
  46.1 15.2 %collective-permute-start.5 = (f32[1,64,128]{2,1,0:T(8,128)S(1)}, f32[1,64,128]{2,1,0:T(8,128)S(1)}, u32[]{:S(2)}, u32[]{:S(2)}) collective-permute-start(f32[1,64,128]{2,1,0:T(8,128)S(1)} %get-tuple-element.42), channel_id=1, source_target_pairs={{1,0},{2,1},{3,2},{4,3},{5,4},{6,5},{7,6},{8,7},{9,8},{10,9},{11,1... | collective-permute-start | bytes 98312 | tf_op jit(solution)/shard_map/ppermute | solution.py:24
  47.5 14.6 %collective-permute-start.6 = (f32[12,16,128]{2,1,0:T(8,128)S(1)}, f32[12,16,128]{2,1,0:T(8,128)S(1)}, u32[]{:S(2)}, u32[]{:S(2)}) collective-permute-start(f32[12,16,128]{2,1,0:T(8,128)S(1)} %get-tuple-element.39), channel_id=1, source_target_pairs={{0,16},{16,32},{32,48},{48,64},{64,80},{80,96},{96,112},{112,128},... | collective-permute-start | bytes 294920 | tf_op jit(solution)/shard_map/ppermute | solution.py:32
  59.2 10.0 %collective-permute-start.7 = (f32[12,16,128]{2,1,0:T(8,128)S(1)}, f32[12,16,128]{2,1,0:T(8,128)S(1)}, u32[]{:S(2)}, u32[]{:S(2)}) collective-permute-start(f32[12,16,128]{2,1,0:T(8,128)S(1)} %get-tuple-element.40), channel_id=1, source_target_pairs={{16,0},{32,16},{48,32},{64,48},{80,64},{96,80},{112,96},{128,112},... | collective-permute-start | bytes 294920 | tf_op jit(solution)/shard_map/ppermute | solution.py:32
  170.5 5.1 %copy-start.12 = (f32[128]{0:T(128)}, f32[128]{0:T(128)S(1)}, u32[]{:S(2)}) copy-start(f32[128]{0:T(128)S(1)} %div.6) | copy-start | bytes 1540
  170.5 11.3 %collective-permute-start.8 = (f32[1,64,128]{2,1,0:T(8,128)S(1)}, f32[1,64,128]{2,1,0:T(8,128)S(1)}, u32[]{:S(2)}, u32[]{:S(2)}) collective-permute-start(f32[1,64,128]{2,1,0:T(8,128)S(1)} %get-tuple-element.33), channel_id=1, source_target_pairs={{0,1},{1,2},{2,3},{3,4},{4,5},{5,6},{6,7},{7,8},{8,9},{9,10},{10,1... | collective-permute-start | bytes 98312 | tf_op jit(solution)/shard_map/ppermute | solution.py:21
  174.2 7.6 %collective-permute-start.9 = (f32[1,64,128]{2,1,0:T(8,128)S(1)}, f32[1,64,128]{2,1,0:T(8,128)S(1)}, u32[]{:S(2)}, u32[]{:S(2)}) collective-permute-start(f32[1,64,128]{2,1,0:T(8,128)S(1)} %get-tuple-element.34), channel_id=1, source_target_pairs={{1,0},{2,1},{3,2},{4,3},{5,4},{6,5},{7,6},{8,7},{9,8},{10,9},{11,1... | collective-permute-start | bytes 98312 | tf_op jit(solution)/shard_map/ppermute | solution.py:24
  176.8 18.4 %all-to-all-start.1 = ((f32[16,64,128]{2,1,0:T(8,128)}), f32[16,64,128]{2,1,0:T(8,128)}, u32[]{:S(2)}, u32[]{:S(2)}) async-start(f32[16,64,128]{2,1,0:T(8,128)} %stack.5), calls=%async_computation.1 | async-start | bytes 1048576 | tf_op jit(solution)/shard_map/all_to_all | solution.py:13
  199.3 12.9 %copy-start.4 = (f32[1,12,64,128]{3,2,1,0:T(8,128)S(1)}, f32[1,12,64,128]{3,2,1,0:T(8,128)}, u32[]{:S(2)}) copy-start(f32[1,12,64,128]{3,2,1,0:T(8,128)} %param.7) | copy-start | bytes 1179652
  199.3 12.9 %collective-permute-start.10 = (f32[1,64,128]{2,1,0:T(8,128)S(1)}, f32[1,64,128]{2,1,0:T(8,128)S(1)}, u32[]{:S(2)}, u32[]{:S(2)}) collective-permute-start(f32[1,64,128]{2,1,0:T(8,128)S(1)} %get-tuple-element.31), channel_id=1, source_target_pairs={{0,1},{1,2},{2,3},{3,4},{4,5},{5,6},{6,7},{7,8},{8,9},{9,10},{10,1... | collective-permute-start | bytes 98312 | tf_op jit(solution)/shard_map/ppermute | solution.py:21
  201.7 10.5 %collective-permute-start.11 = (f32[1,64,128]{2,1,0:T(8,128)S(1)}, f32[1,64,128]{2,1,0:T(8,128)S(1)}, u32[]{:S(2)}, u32[]{:S(2)}) collective-permute-start(f32[1,64,128]{2,1,0:T(8,128)S(1)} %get-tuple-element.32), channel_id=1, source_target_pairs={{1,0},{2,1},{3,2},{4,3},{5,4},{6,5},{7,6},{8,7},{9,8},{10,9},{11,1... | collective-permute-start | bytes 98312 | tf_op jit(solution)/shard_map/ppermute | solution.py:24
  203.0 10.0 %collective-permute-start.12 = (f32[12,16,128]{2,1,0:T(8,128)S(1)}, f32[12,16,128]{2,1,0:T(8,128)S(1)}, u32[]{:S(2)}, u32[]{:S(2)}) collective-permute-start(f32[12,16,128]{2,1,0:T(8,128)S(1)} %get-tuple-element.29), channel_id=1, source_target_pairs={{0,16},{16,32},{32,48},{48,64},{64,80},{80,96},{96,112},{112,128},... | collective-permute-start | bytes 294920 | tf_op jit(solution)/shard_map/ppermute | solution.py:32
  210.3 9.8 %collective-permute-start.13 = (f32[12,16,128]{2,1,0:T(8,128)S(1)}, f32[12,16,128]{2,1,0:T(8,128)S(1)}, u32[]{:S(2)}, u32[]{:S(2)}) collective-permute-start(f32[12,16,128]{2,1,0:T(8,128)S(1)} %get-tuple-element.30), channel_id=1, source_target_pairs={{16,0},{32,16},{48,32},{64,48},{80,64},{96,80},{112,96},{128,112},... | collective-permute-start | bytes 294920 | tf_op jit(solution)/shard_map/ppermute | solution.py:32
  (6 other events, 11.3 us)
